TPU v7x, 32 devices: a whole 2x2x4 slice. The times are simulated.
32 devices in a mesh: groups: 2 (over x), gx: 16 (over z, y, core).
Axes of the slice: x: 2, y: 2, z: 4, core: 2. Of those that a mesh axis runs over, the one named last changes fastest.
Arguments:
- velocity: bfloat16 [3, 16, 128, 128], P(None, 'groups', 'gx'), parts along dimension 1, may hold values from -5 to 5
- offsets: int32 [6], P('groups'), parts along dimension 0, may hold values from 0 to 1023
- conv_in: bfloat16 [64, 9, 3, 3], replicated, may hold values from -0.625 to 0.625
- conv_mid: bfloat16 [64, 64, 3, 3], replicated, may hold values from -0.25 to 0.25
- conv_out: bfloat16 [36, 64, 3, 3], replicated, may hold values from -0.25 to 0.25
- cotangent: float32 [3, 8, 128, 128], P(None, 'groups', 'gx'), parts along dimension 1, may hold values from -6 to 6
Outputs:
- final_state: float32 [3, 8, 128, 128], P(None, 'groups', 'gx'), parts along dimension 1
- weight_grads: bfloat16 [36, 8, 128, 128], P(None, 'groups', 'gx'), parts along dimension 1
There are 2 independent parts, one for each index of `groups`. A program takes and returns all parts, laid end to end along the dimension named above; an argument that names none is the same for every part. Nothing has to cross between parts.
All inputs are finite; a program needn't handle non-finite values.
Results may differ from a plain program's by a relative error of at most 0.0045.
Values may be sent and summed in bfloat16 or wider, within the bound.
No kernel may reach another device: no remote copies, remote signals or barrier semaphores. Data moves between devices by JAX's collectives and lax.ppermute only.
A program may use at most 128 MiB of HBM per device.

v0:
```python
import math
import jax
import jax.numpy as jnp
from jax import lax
from jax.sharding import PartitionSpec as P

DOMAIN = 1024
SPREAD = 0.25
STEP_SIZE = 0.3
BASE_TAPS = (-0.0625, 0.5625, 0.5625, -0.0625)


def with_halo(shard, sides, width):
    for axis, dim in sides:
        size, length = (lax.axis_size(axis), shard.shape[dim])
        up = [(i, (i + 1) % size) for i in range(size)]
        down = [(j, i) for i, j in up]
        last = lax.slice_in_dim(shard, length - width, length, axis=dim)
        leading = lax.slice_in_dim(shard, 0, width, axis=dim)
        before = lax.ppermute(last, axis, up)
        after = lax.ppermute(leading, axis, down)
        shard = jnp.concatenate([before, shard, after], axis=dim)
    return shard


def shortened(shard):

    def short(part):
        return part.astype(jnp.bfloat16) if part.dtype == jnp.float32 else part

    return jax.tree.map(short, shard)


def phase_angle(coords, offset):
    return (coords + offset).astype(jnp.float32) * (2.0 * math.pi / DOMAIN)


def positions(zcoord, ycoord, xcoord, offsets):
    angle_z = phase_angle(zcoord, offsets[2])[:, None, None]
    angle_y = phase_angle(ycoord, offsets[1])
    angle_x = phase_angle(xcoord, offsets[0])
    angle_y = angle_y[None, :, None]
    angle_x = angle_x[None, None, :]
    zero_grid = jnp.zeros_like(angle_z + angle_y + angle_x)
    channel_list = [
        jnp.sin(angle_x),
        jnp.cos(angle_x),
        jnp.sin(angle_y),
        jnp.cos(angle_y),
        jnp.sin(angle_z),
        jnp.cos(angle_z),
    ]
    return jnp.stack([item + zero_grid for item in channel_list], axis=0)


def wrap_pad(values, margin, axis_list):
    for roll_axis in axis_list:
        extent = values.shape[roll_axis]
        values = jnp.concatenate(
            [
                lax.slice_in_dim(values, extent - margin, extent, axis=roll_axis),
                values,
                lax.slice_in_dim(values, 0, margin, axis=roll_axis),
            ],
            axis=roll_axis,
        )
    return values


def conv_layer(inputs, kernel, kernel_layout):
    return lax.conv_general_dilated(
        inputs,
        kernel,
        (1, 1),
        "VALID",
        dimension_numbers=("CNHW", kernel_layout, "CNHW"),
        preferred_element_type=jnp.float32,
    )


def interpolation(raw_output):
    grouped = raw_output.reshape((3, 3, 4) + raw_output.shape[1:])
    base_taps = jnp.array(BASE_TAPS, dtype=jnp.float32).reshape(
        (1, 1, 4) + (1,) * (raw_output.ndim - 1)
    )
    mixed = base_taps + SPREAD * (grouped - jnp.mean(grouped, axis=2, keepdims=True))
    return mixed.reshape(raw_output.shape).astype(jnp.bfloat16)


def network(inputs, conv_in, conv_mid, conv_out, kernel_layout):
    first = jax.nn.gelu(conv_layer(inputs, conv_in, kernel_layout)).astype(jnp.bfloat16)
    second = jax.nn.gelu(conv_layer(first, conv_mid, kernel_layout)).astype(jnp.bfloat16)
    return interpolation(conv_layer(second, conv_out, kernel_layout))


def advect(padded, weights, row_direction):
    rows = padded.shape[2] - 4
    depth = padded.shape[1] - 4
    middle = padded[:, 2 : 2 + depth, 2 : 2 + rows]
    grouped = weights.reshape((3, 3, 4) + middle.shape[1:])
    change = jnp.zeros_like(middle)
    for direction in (0, 1, 2):
        nearby = {}
        for offset in (-2, -1, 0, 1, 2):
            if direction == 2:
                nearby[offset] = padded[:, 2 + offset : 2 + offset + depth, 2 : 2 + rows]
            elif direction == row_direction:
                nearby[offset] = padded[:, 2 : 2 + depth, 2 + offset : 2 + offset + rows]
            else:
                nearby[offset] = jnp.roll(middle, -offset, axis=3)
        speed_up = 0.5 * (middle[direction] + nearby[1][direction])
        speed_down = 0.5 * (middle[direction] + nearby[-1][direction])
        face_up = sum(
            (grouped[:, direction, tap_index] * nearby[tap_index - 1] for tap_index in range(4))
        )
        face_down = sum(
            (grouped[:, direction, tap_index] * nearby[tap_index - 2] for tap_index in range(4))
        )
        change = change + speed_up * face_up - speed_down * face_down
    return middle - STEP_SIZE * change


def halo_rows(values):
    return with_halo(values, (("gx", 2),), 2)


def on_device(velocity, offsets, conv_in, conv_mid, conv_out, cotangent):
    depth = velocity.shape[1] - 4
    row_count = velocity.shape[2]
    devices = lax.axis_size("gx")
    position = lax.axis_index("gx")
    total_cells = row_count * devices
    zcoord = jnp.arange(depth, dtype=jnp.int32)
    extended = with_halo(velocity[:, 2 : 2 + depth], (("gx", 2),), 3)
    ycoord = (position * row_count - 3 + jnp.arange(row_count + 6, dtype=jnp.int32)) % total_cells
    xcoord = (jnp.arange(total_cells + 6, dtype=jnp.int32) - 3) % total_cells
    features = positions(zcoord, ycoord, xcoord, offsets).astype(jnp.bfloat16)
    inputs = jnp.concatenate([wrap_pad(extended, 3, (3,)), features], axis=0)
    stencil = network(inputs, conv_in, conv_mid, conv_out, "OIHW")
    row_direction = 1
    block_cotangent = jnp.swapaxes(
        lax.all_to_all(cotangent, "gx", split_axis=3, concat_axis=2, tiled=True), 2, 3
    )
    weights = stencil.astype(jnp.float32)
    start = velocity.astype(jnp.float32)
    ghost_low = start[:, :2]
    ghost_high = start[:, 2 + depth :]

    def step(padded, weight_values):
        return advect(padded, weight_values, row_direction)

    padded_start = halo_rows(start)
    middle, pull_first = jax.vjp(step, padded_start, weights)
    padded_middle = halo_rows(jnp.concatenate([ghost_low, middle, ghost_high], axis=1))
    block_final, pull_second = jax.vjp(step, padded_middle, weights)
    back_padded, grad_second = pull_second(block_cotangent)
    back_inner = back_padded[:, 2 : 2 + depth]
    rim_rows = jnp.concatenate([back_inner[:, :, :2], back_inner[:, :, -2:]], axis=2)
    beside_all = with_halo(shortened(rim_rows), (("gx", 2),), 2).astype(rim_rows.dtype)
    middle_grad = jnp.concatenate(
        [
            back_inner[:, :, 2:4] + beside_all[:, :, :2],
            back_inner[:, :, 4:-4],
            back_inner[:, :, -4:-2] + beside_all[:, :, -2:],
        ],
        axis=2,
    )
    unused_grad, grad_first = pull_first(middle_grad)
    weight_grads = (grad_first + grad_second).astype(jnp.bfloat16)
    final_state = jnp.swapaxes(
        lax.all_to_all(block_final, "gx", split_axis=3, concat_axis=2, tiled=True), 2, 3
    )
    return (final_state, weight_grads)


def solution(mesh):
    return jax.shard_map(
        on_device,
        mesh=mesh,
        in_specs=(
            P(None, "groups", "gx", None),
            P("groups"),
            P(),
            P(),
            P(),
            P(None, "groups", "gx", None),
        ),
        out_specs=(P(None, "groups", "gx", None), P(None, "groups", "gx", None)),
        check_vma=False,
    )
```

profile of v0, /device:TPU:0, one launch (start us, length us, event | category | flops | bytes accessed | tf_op | source)
XLA Modules:
  0.0 85.5 jit_solution(15485054560610476140)
XLA Ops:
  0.7 0.8 fusion.143
  2.0 5.1 %collective-permute-start.1 = (bf16[3,4,3,128]{3,2,1,0:T(4,128)(2,1)S(1)}, bf16[3,4,3,128]{3,2,1,0:T(4,128)(2,1)S(1)}, u32[]{:S(2)}, u32[]{:S(2)}) collective-permute-start(bf16[3,4,3,128]{3,2,1,0:T(4,128)(2,1)S(1)} %get-tuple-element.171), channel_id=1, source_target_pairs={{1,0},{2,1},{3,2},{4,3},{5,4},{6,5},{7,6},{8,7},{9,8},{10,9},{11,1... | collective-permute-start | bytes 27656 | tf_op jit(solution)/shard_map/ppermute | solution.py:21
  7.1 1.5 %fusion.141 = (f32[3,8,2,128]{3,2,1,0:T(2,128)}, f32[3,8,2,128]{3,2,1,0:T(2,128)}) fusion(bf16[3,8,8,128]{3,2,1,0:T(8,128)(2,1)} %param.7), kind=kLoop, calls=%fused_computation.326 | loop fusion | bytes 98304 | tf_op jit(solution)/shard_map/slice | solution.py:19
  9.3 1.1 %copy.106 = f32[3,4,8,128]{2,1,0,3:T(4,128)S(1)} copy(f32[3,4,8,128]{3,2,1,0:T(8,128)} %param.12) | data formatting | bytes 98304 | tf_op args[5]
  10.4 1.4 %reshape.458 = f32[16,1,768]{2,1,0:T(1,128)} reshape(f32[128,3,4,8]{3,2,1,0:T(4,128)S(1)} %bitcast.472) | data formatting | bytes 98304
  11.8 5.9 %all-to-all-start.1 = ((f32[16,1,768]{2,1,0:T(1,128)}), f32[16,1,768]{2,1,0:T(1,128)}, u32[]{:S(2)}, u32[]{:S(2)}) async-start(f32[16,1,768]{2,1,0:T(1,128)} %reshape.458), calls=%async_computation.1 | async-start | bytes 98304 | tf_op jit(solution)/shard_map/all_to_all | solution.py:142
  17.7 0.8 convert_element_type.54
  18.5 1.5 %fusion.144 = (f32[3,4,8,1]{3,2,1,0:T(8,128)}, f32[3,4,8,1]{3,2,1,0:T(8,128)S(1)}) fusion(bf16[3,8,8,128]{3,2,1,0:T(8,128)(2,1)} %param.7), kind=kLoop, calls=%fused_computation.329 | loop fusion | bytes 1536 | tf_op jit(solution)/shard_map/jvp(jit(_roll_static))/slice | solution.py:110
  28.6 0.8 reshape.440
  30.4 1.9 %copy.88 = bf16[9,14,32,19]{2,0,3,1:T(8,128)(2,1)S(1)} copy(bf16[9,14,32,19]{3,2,1,0:T(8,128)(2,1)S(1)} %fusion.36) | data formatting | bytes 306432 | tf_op jit(solution)/shard_map/conv_general_dilated | solution.py:71
  32.3 4.4 %select_bitcast_fusion = bf16[12,4,8,17,64]{4,2,1,3,0:T(8,128)(2,1)S(1)} fusion(pred[32,17]{0,1:T(8,128)(4,1)S(1)} %copy-done.23, bf16[9,14,32,19]{2,0,3,1:T(8,128)(2,1)S(1)} %copy.88, bf16[64,9,3,3]{0,3,2,1:T(4,128)(2,1)} %param.9), kind=kOutput, calls=%fused_computation.30 | convolution fusion | flops 72278016 | bytes 999712 | tf_op jit(solution)/shard_map/conv_general_dilated | solution.py:71
  36.9 4.0 %select_bitcast_fusion.1 = bf16[10,4,8,17,64]{4,2,1,3,0:T(8,128)(2,1)S(1)} fusion(pred[32,17]{0,1:T(8,128)(4,1)S(1)} %copy-done.22, bf16[64,64,3,3]{1,0,3,2:T(8,128)(2,1)S(1)} %copy-done, bf16[12,4,7,2,64]{4,2,1,3,0:T(8,128)(2,1)S(1)} %slice.444, bf16[12,4,8,17,64]{4,2,1,3,0:T(8,128)(2,1)S(1)} %select_bitcast_fusion), kind=kOutput, calls=%fused_computation.37 | convolution fusion | flops 407363584 | bytes 1692192 | tf_op jit(solution)/shard_map/conv_general_dilated | solution.py:71
  40.9 2.9 %fusion.28 = f32[8,32,17,36]{3,1,2,0:T(8,128)S(1)} fusion(bf16[36,64,3,3]{1,0,3,2:T(8,128)(2,1)S(1)} %copy-done.21, bf16[10,4,7,2,64]{4,2,1,3,0:T(8,128)(2,1)S(1)} %slice.445, bf16[10,4,8,17,64]{4,2,1,3,0:T(8,128)(2,1)S(1)} %select_bitcast_fusion.1), kind=kOutput, calls=%fused_computation.33 | convolution fusion | flops 182820864 | bytes 1436160 | tf_op jit(solution)/shard_map/conv_general_dilated | solution.py:71
  43.8 1.3 %copy.90 = f32[8,32,17,36]{3,0,2,1:T(8,128)S(1)} copy(f32[8,32,17,36]{3,1,2,0:T(8,128)S(1)} %fusion.28) | data formatting | bytes 1253376 | tf_op jit(solution)/shard_map/conv_general_dilated | solution.py:71
  45.2 0.9 %copy.116 = f32[8,4,128,36]{2,0,1,3:T(8,128)S(1)} copy(f32[8,4,128,36]{3,0,2,1:T(8,128)S(1)} %slice.446) | data formatting | bytes 1179648
  46.9 1.3 %broadcast_multiply_fusion.1 = (f32[4,8,128]{2,1,0:T(8,128)S(1)}, f32[4,8,128]{2,1,0:T(8,128)S(1)}, f32[4,8,128]{2,1,0:T(8,128)S(1)}, f32[4,8,128]{2,1,0:T(8,128...) fusion(f32[3,4,8,1]{3,2,1,0:T(8,128)S(1)} %get-tuple-element.173, f32[3,4,8,127]{3,2,1,0:T(8,128)S(1)} %get-tuple-element.175, ...), kind=kLoop, calls=%fused_computation.273 | loop fusion | flops 45056 | bytes 385024 | tf_op jit(solution)/shard_map/transpose(jvp())/mul | solution.py:119
  48.2 0.8 fusion.86
  49.0 1.0 %fusion.57 = f32[3,4,8,128]{3,2,1,0:T(8,128)S(1)} fusion(f32[3,4,8,2]{3,2,1,0:T(8,128)S(1)} %copy-done.5, f32[3,4,8,126]{3,2,1,0:T(8,128)S(1)} %copy-done.7, f32[3,4,8,126]{3,2,1,0:T(8,128)S(1)} %copy-done.6, f32[3,4,8,2]{3,2,1,0:T(8,128)S(1)} %copy-done.4, f32[3,8,8,128]{3,2,1,0:T(8,128)S(1)} %convert_element_type.54, ...), kind=kLoop, calls=%fused_computation.113 | loop fusion | flops 774144 | bytes 1523712 | tf_op jit(solution)/shard_map/jvp()/sub | solution.py:120
  50.2 4.4 %collective-permute-start.4 = (f32[3,8,2,128]{3,2,1,0:T(2,128)S(1)}, f32[3,8,2,128]{3,2,1,0:T(2,128)S(1)}, u32[]{:S(2)}, u32[]{:S(2)}) collective-permute-start(f32[3,8,2,128]{3,2,1,0:T(2,128)S(1)} %get-tuple-element.111), channel_id=1, source_target_pairs={{1,0},{2,1},{3,2},{4,3},{5,4},{6,5},{7,6},{8,7},{9,8},{10,9},{11,1... | collective-permute-start | bytes 73736 | tf_op jit(solution)/shard_map/ppermute | solution.py:21
  54.7 1.4 %collective-permute-done.4 = f32[3,8,2,128]{3,2,1,0:T(2,128)S(1)} collective-permute-done((f32[3,8,2,128]{3,2,1,0:T(2,128)S(1)}, f32[3,8,2,128]{3,2,1,0:T(2,128)S(1)}, u32[]{:S(2)}, u32[]{:S(2)}) %collective-permute-start.4) | collective-permute-done | bytes 24608 | tf_op jit(solution)/shard_map/ppermute | solution.py:21
  56.2 4.4 %collective-permute-done.5 = f32[3,8,2,128]{3,2,1,0:T(2,128)S(1)} collective-permute-done((f32[3,8,2,128]{3,2,1,0:T(2,128)S(1)}, f32[3,8,2,128]{3,2,1,0:T(2,128)S(1)}, u32[]{:S(2)}, u32[]{:S(2)}) %collective-permute-start.5) | collective-permute-done | bytes 24608 | tf_op jit(solution)/shard_map/ppermute | solution.py:20
  61.2 1.5 %reduce = f32[16,768]{1,0:T(8,128)S(1)} reduce(f32[16,1,768]{2,1,0:T(1,128)} %all-to-all-done.1, f32[]{:T(128)} %broadcast.630), dimensions={1}, to_apply=%all_to_all.30.reduce_sub_computation | reduce | bytes 98308 | tf_op jit(solution)/shard_map/all_to_all | solution.py:142
  62.8 0.9 %reshape.459 = f32[128,3,4,8]{3,2,1,0:T(4,128)S(1)} reshape(f32[16,768]{1,0:T(8,128)S(1)} %reduce) | data formatting | bytes 98304
  65.8 4.4 %collective-permute-start.7 = (bf16[3,4,2,128]{3,2,1,0:T(2,128)(2,1)S(1)}, bf16[3,4,2,128]{3,2,1,0:T(2,128)(2,1)}, u32[]{:S(2)}, u32[]{:S(2)}) collective-permute-start(bf16[3,4,2,128]{3,2,1,0:T(2,128)(2,1)S(1)} %get-tuple-element.95), channel_id=1, source_target_pairs={{1,0},{2,1},{3,2},{4,3},{5,4},{6,5},{7,6},{8,7},{9,8},{10,9},{11,1... | collective-permute-start | bytes 18440 | tf_op jit(solution)/shard_map/ppermute | solution.py:21
  70.7 1.4 %reshape.456 = f32[16,1,768]{2,1,0:T(1,128)} reshape(f32[128,3,4,8]{3,2,1,0:T(4,128)S(1)} %bitcast.469) | data formatting | bytes 98304
  72.1 3.5 %all-to-all-start = ((f32[16,1,768]{2,1,0:T(1,128)}), f32[16,1,768]{2,1,0:T(1,128)S(1)}, u32[]{:S(2)}, u32[]{:S(2)}) async-start(f32[16,1,768]{2,1,0:T(1,128)} %reshape.456), calls=%async_computation | async-start | bytes 98304 | tf_op jit(solution)/shard_map/all_to_all | solution.py:171
  75.8 0.8 convert_add_fusion
  77.1 0.8 multiply_bitcast_fusion.29
  77.9 0.8 multiply_bitcast_fusion.31
  80.0 2.4 %all-to-all-done = f32[16,1,768]{2,1,0:T(1,128)S(1)} async-done(((f32[16,1,768]{2,1,0:T(1,128)}), f32[16,1,768]{2,1,0:T(1,128)S(1)}, u32[]{:S(2)}, u32[]{:S(2)}) %all-to-all-start) | async-done | bytes 49184 | tf_op jit(solution)/shard_map/all_to_all | solution.py:171
  83.1 0.9 %reshape.457 = f32[128,3,4,8]{3,2,1,0:T(4,128)S(1)} reshape(f32[16,768]{1,0:T(8,128)S(1)} %reduce.1) | data formatting | bytes 98304
  84.5 0.9 %all_to_all.29 = f32[3,4,128,8]{2,3,1,0:T(8,128)} reshape(f32[3,4,16,8,8]{3,2,4,1,0:T(8,128)S(1)} %bitcast.471) | data formatting | bytes 98304 | tf_op jit(solution)/shard_map/all_to_all | solution.py:171
  (136 shorter events, 17.9 us)
Async XLA Ops:
  0.6 36.2 %copy-start = (bf16[64,64,3,3]{1,0,3,2:T(8,128)(2,1)S(1)}, bf16[64,64,3,3]{1,0,3,2:T(8,128)(2,1)}, u32[]{:S(2)}) copy-start(bf16[64,64,3,3]{1,0,3,2:T(8,128)(2,1)} %param.10) | copy-start | bytes 221188
  0.6 27.0 %copy-start.20 = (f32[4]{0:T(128)S(1)}, f32[4]{0:T(128)}, u32[]{:S(2)}) copy-start(f32[4]{0:T(128)} %constant.69.clone) | copy-start | bytes 52
  0.7 19.4 %copy-start.1 = (bf16[3,8,8,128]{3,2,1,0:T(8,128)(2,1)S(1)}, bf16[3,8,8,128]{3,2,1,0:T(8,128)(2,1)}, u32[]{:S(2)}) copy-start(bf16[3,8,8,128]{3,2,1,0:T(8,128)(2,1)} %param.7) | copy-start | bytes 147460
  0.7 24.2 %copy-start.19 = (s32[3]{0:T(128)S(1)}, s32[3]{0:T(128)}, u32[]{:S(2)}) copy-start(s32[3]{0:T(128)} %param.8) | copy-start | bytes 40
  1.5 26.2 %collective-permute-start = (bf16[3,4,3,128]{3,2,1,0:T(4,128)(2,1)S(1)}, bf16[3,4,3,128]{3,2,1,0:T(4,128)(2,1)S(1)}, u32[]{:S(2)}, u32[]{:S(2)}) collective-permute-start(bf16[3,4,3,128]{3,2,1,0:T(4,128)(2,1)S(1)} %get-tuple-element.170), channel_id=1, source_target_pairs={{0,1},{1,2},{2,3},{3,4},{4,5},{5,6},{6,7},{7,8},{8,9},{9,10},{10,1... | collective-permute-start | bytes 27656 | tf_op jit(solution)/shard_map/ppermute | solution.py:20
  2.0 25.7 %collective-permute-start.1 = (bf16[3,4,3,128]{3,2,1,0:T(4,128)(2,1)S(1)}, bf16[3,4,3,128]{3,2,1,0:T(4,128)(2,1)S(1)}, u32[]{:S(2)}, u32[]{:S(2)}) collective-permute-start(bf16[3,4,3,128]{3,2,1,0:T(4,128)(2,1)S(1)} %get-tuple-element.171), channel_id=1, source_target_pairs={{1,0},{2,1},{3,2},{4,3},{5,4},{6,5},{7,6},{8,7},{9,8},{10,9},{11,1... | collective-permute-start | bytes 27656 | tf_op jit(solution)/shard_map/ppermute | solution.py:21
  8.6 38.3 %collective-permute-start.2 = (f32[3,8,2,128]{3,2,1,0:T(2,128)}, f32[3,8,2,128]{3,2,1,0:T(2,128)}, u32[]{:S(2)}, u32[]{:S(2)}) collective-permute-start(f32[3,8,2,128]{3,2,1,0:T(2,128)} %get-tuple-element.166), channel_id=1, source_target_pairs={{1,0},{2,1},{3,2},{4,3},{5,4},{6,5},{7,6},{8,7},{9,8},{10,9},{11,1... | collective-permute-start | bytes 73736 | tf_op jit(solution)/shard_map/ppermute | solution.py:21
  9.3 38.9 %collective-permute-start.3 = (f32[3,8,2,128]{3,2,1,0:T(2,128)}, f32[3,8,2,128]{3,2,1,0:T(2,128)}, u32[]{:S(2)}, u32[]{:S(2)}) collective-permute-start(f32[3,8,2,128]{3,2,1,0:T(2,128)} %get-tuple-element.167), channel_id=1, source_target_pairs={{0,1},{1,2},{2,3},{3,4},{4,5},{5,6},{6,7},{7,8},{8,9},{9,10},{10,1... | collective-permute-start | bytes 73736 | tf_op jit(solution)/shard_map/ppermute | solution.py:20
  11.8 48.9 %all-to-all-start.1 = ((f32[16,1,768]{2,1,0:T(1,128)}), f32[16,1,768]{2,1,0:T(1,128)}, u32[]{:S(2)}, u32[]{:S(2)}) async-start(f32[16,1,768]{2,1,0:T(1,128)} %reshape.458), calls=%async_computation.1 | async-start | bytes 98304 | tf_op jit(solution)/shard_map/all_to_all | solution.py:142
  29.7 2.6 %copy-start.23 = (pred[32,17]{0,1:T(8,128)(4,1)S(1)}, pred[32,17]{0,1:T(8,128)(4,1)}, u32[]{:S(2)}) copy-start(pred[32,17]{0,1:T(8,128)(4,1)} %constant.230) | copy-start | bytes 1636
  32.3 4.5 %copy-start.22 = (pred[32,17]{0,1:T(8,128)(4,1)S(1)}, pred[32,17]{0,1:T(8,128)(4,1)}, u32[]{:S(2)}) copy-start(pred[32,17]{0,1:T(8,128)(4,1)} %constant.229) | copy-start | bytes 1636
  36.8 4.0 %copy-start.21 = (bf16[36,64,3,3]{1,0,3,2:T(8,128)(2,1)S(1)}, bf16[36,64,3,3]{1,0,3,2:T(8,128)(2,1)}, u32[]{:S(2)}) copy-start(bf16[36,64,3,3]{1,0,3,2:T(8,128)(2,1)} %param.11) | copy-start | bytes 124420
  46.2 2.8 %copy-start.4 = (f32[3,4,8,2]{3,2,1,0:T(8,128)S(1)}, f32[3,4,8,2]{3,2,1,0:T(8,128)}, u32[]{:S(2)}) copy-start(f32[3,4,8,2]{3,2,1,0:T(8,128)} %get-tuple-element.176) | copy-start | bytes 2308
  46.2 2.8 %copy-start.5 = (f32[3,4,8,2]{3,2,1,0:T(8,128)S(1)}, f32[3,4,8,2]{3,2,1,0:T(8,128)}, u32[]{:S(2)}) copy-start(f32[3,4,8,2]{3,2,1,0:T(8,128)} %get-tuple-element.177) | copy-start | bytes 2308
  46.2 2.8 %copy-start.6 = (f32[3,4,8,126]{3,2,1,0:T(8,128)S(1)}, f32[3,4,8,126]{3,2,1,0:T(8,128)}, u32[]{:S(2)}) copy-start(f32[3,4,8,126]{3,2,1,0:T(8,128)} %get-tuple-element.178) | copy-start | bytes 145156
  46.2 2.8 %copy-start.7 = (f32[3,4,8,126]{3,2,1,0:T(8,128)S(1)}, f32[3,4,8,126]{3,2,1,0:T(8,128)}, u32[]{:S(2)}) copy-start(f32[3,4,8,126]{3,2,1,0:T(8,128)} %get-tuple-element.179) | copy-start | bytes 145156
  48.9 7.2 %copy-start.16 = (f32[4,8,128]{2,1,0:T(8,128)}, f32[4,8,128]{2,1,0:T(8,128)S(1)}, u32[]{:S(2)}) copy-start(f32[4,8,128]{2,1,0:T(8,128)S(1)} %get-tuple-element.117) | copy-start | bytes 49156
  50.2 5.9 %collective-permute-start.4 = (f32[3,8,2,128]{3,2,1,0:T(2,128)S(1)}, f32[3,8,2,128]{3,2,1,0:T(2,128)S(1)}, u32[]{:S(2)}, u32[]{:S(2)}) collective-permute-start(f32[3,8,2,128]{3,2,1,0:T(2,128)S(1)} %get-tuple-element.111), channel_id=1, source_target_pairs={{1,0},{2,1},{3,2},{4,3},{5,4},{6,5},{7,6},{8,7},{9,8},{10,9},{11,1... | collective-permute-start | bytes 73736 | tf_op jit(solution)/shard_map/ppermute | solution.py:21
  54.7 6.0 %collective-permute-start.5 = (f32[3,8,2,128]{3,2,1,0:T(2,128)S(1)}, f32[3,8,2,128]{3,2,1,0:T(2,128)S(1)}, u32[]{:S(2)}, u32[]{:S(2)}) collective-permute-start(f32[3,8,2,128]{3,2,1,0:T(2,128)S(1)} %get-tuple-element.110), channel_id=1, source_target_pairs={{0,1},{1,2},{2,3},{3,4},{4,5},{5,6},{6,7},{7,8},{8,9},{9,10},{10,1... | collective-permute-start | bytes 73736 | tf_op jit(solution)/shard_map/ppermute | solution.py:20
  65.6 11.0 %copy-start.17 = (f32[4,8,128]{2,1,0:T(8,128)S(1)}, f32[4,8,128]{2,1,0:T(8,128)}, u32[]{:S(2)}) copy-start(f32[4,8,128]{2,1,0:T(8,128)} %copy-done.16) | copy-start | bytes 49156
  65.6 11.1 %copy-start.18 = (f32[4,8,128]{2,1,0:T(8,128)S(1)}, f32[4,8,128]{2,1,0:T(8,128)}, u32[]{:S(2)}) copy-start(f32[4,8,128]{2,1,0:T(8,128)} %get-tuple-element.114) | copy-start | bytes 49156
  65.7 10.0 %collective-permute-start.6 = (bf16[3,4,2,128]{3,2,1,0:T(2,128)(2,1)S(1)}, bf16[3,4,2,128]{3,2,1,0:T(2,128)(2,1)}, u32[]{:S(2)}, u32[]{:S(2)}) collective-permute-start(bf16[3,4,2,128]{3,2,1,0:T(2,128)(2,1)S(1)} %get-tuple-element.94), channel_id=1, source_target_pairs={{0,1},{1,2},{2,3},{3,4},{4,5},{5,6},{6,7},{7,8},{8,9},{9,10},{10,1... | collective-permute-start | bytes 18440 | tf_op jit(solution)/shard_map/ppermute | solution.py:20
  65.8 9.9 %collective-permute-start.7 = (bf16[3,4,2,128]{3,2,1,0:T(2,128)(2,1)S(1)}, bf16[3,4,2,128]{3,2,1,0:T(2,128)(2,1)}, u32[]{:S(2)}, u32[]{:S(2)}) collective-permute-start(bf16[3,4,2,128]{3,2,1,0:T(2,128)(2,1)S(1)} %get-tuple-element.95), channel_id=1, source_target_pairs={{1,0},{2,1},{3,2},{4,3},{5,4},{6,5},{7,6},{8,7},{9,8},{10,9},{11,1... | collective-permute-start | bytes 18440 | tf_op jit(solution)/shard_map/ppermute | solution.py:21
  70.3 6.5 %copy-start.12 = (f32[3,1,1,4,8,2]{5,4,3,0,2,1:T(8,128)S(1)}, f32[3,1,1,4,8,2]{5,4,3,0,2,1:T(8,128)}, u32[]{:S(2)}) copy-start(f32[3,1,1,4,8,2]{5,4,3,0,2,1:T(8,128)} %get-tuple-element.86) | copy-start | bytes 2308
  70.3 6.5 %copy-start.13 = (f32[3,1,1,4,8,126]{5,4,3,0,2,1:T(8,128)S(1)}, f32[3,1,1,4,8,126]{5,4,3,0,2,1:T(8,128)}, u32[]{:S(2)}) copy-start(f32[3,1,1,4,8,126]{5,4,3,0,2,1:T(8,128)} %get-tuple-element.88) | copy-start | bytes 145156
  70.3 6.5 %copy-start.14 = (f32[3,1,1,4,8,127]{5,4,3,0,2,1:T(8,128)S(1)}, f32[3,1,1,4,8,127]{5,4,3,0,2,1:T(8,128)}, u32[]{:S(2)}) copy-start(f32[3,1,1,4,8,127]{5,4,3,0,2,1:T(8,128)} %get-tuple-element.90) | copy-start | bytes 146308
  70.3 6.5 %copy-start.15 = (f32[3,1,1,4,8,1]{5,4,3,0,2,1:T(8,128)S(1)}, f32[3,1,1,4,8,1]{5,4,3,0,2,1:T(8,128)}, u32[]{:S(2)}) copy-start(f32[3,1,1,4,8,1]{5,4,3,0,2,1:T(8,128)} %get-tuple-element.92) | copy-start | bytes 1156
  70.3 6.6 %copy-start.8 = (f32[3,1,1,4,8,2]{5,4,3,0,2,1:T(8,128)S(1)}, f32[3,1,1,4,8,2]{5,4,3,0,2,1:T(8,128)}, u32[]{:S(2)}) copy-start(f32[3,1,1,4,8,2]{5,4,3,0,2,1:T(8,128)} %get-tuple-element.87) | copy-start | bytes 2308
  70.3 6.6 %copy-start.9 = (f32[3,1,1,4,8,126]{5,4,3,0,2,1:T(8,128)S(1)}, f32[3,1,1,4,8,126]{5,4,3,0,2,1:T(8,128)}, u32[]{:S(2)}) copy-start(f32[3,1,1,4,8,126]{5,4,3,0,2,1:T(8,128)} %get-tuple-element.89) | copy-start | bytes 145156
  70.3 6.6 %copy-start.10 = (f32[3,1,1,4,8,127]{5,4,3,0,2,1:T(8,128)S(1)}, f32[3,1,1,4,8,127]{5,4,3,0,2,1:T(8,128)}, u32[]{:S(2)}) copy-start(f32[3,1,1,4,8,127]{5,4,3,0,2,1:T(8,128)} %get-tuple-element.91) | copy-start | bytes 146308
  70.3 6.6 %copy-start.11 = (f32[3,1,1,4,8,1]{5,4,3,0,2,1:T(8,128)S(1)}, f32[3,1,1,4,8,1]{5,4,3,0,2,1:T(8,128)}, u32[]{:S(2)}) copy-start(f32[3,1,1,4,8,1]{5,4,3,0,2,1:T(8,128)} %get-tuple-element.93) | copy-start | bytes 1156
  72.1 10.2 %all-to-all-start = ((f32[16,1,768]{2,1,0:T(1,128)}), f32[16,1,768]{2,1,0:T(1,128)S(1)}, u32[]{:S(2)}, u32[]{:S(2)}) async-start(f32[16,1,768]{2,1,0:T(1,128)} %reshape.456), calls=%async_computation | async-start | bytes 98304 | tf_op jit(solution)/shard_map/all_to_all | solution.py:171
  (2 other events, 4.1 us)
where the time goes:
time: 86.4 us; the launch traced here: 85.5 us
  local copies, waits for them, and re-layouts  26.2 us (30%)
  starting transfers between devices  24.5 us (28%)
  other arithmetic  13.9 us (16%)
  matrix products  11.3 us (13%)
  waiting for transfers between devices  8.24 us (10%)
  between operations  1.44 us (2%)
    ppermute x4, starting transfers between devices, with_halo(): after = lax.ppermute(leading, axis, down)  14.5 us
    conv_general_dilated x3, matrix products, conv_layer(): lax.conv_general_dilated(inputs, kernel, (1, 1), 'VALID', dimension_numbe...  11.3 us
    unnamed x60, local copies, waits for them, and re-layouts  7.5 us
    all_to_all x1, starting transfers between devices, on_device(): lax.all_to_all(cotangent, 'gx', split_axis=3, concat_axis=2, tiled=True)  5.86 us
    ppermute x4, waiting for transfers between devices, with_halo(): before = lax.ppermute(last, axis, up)  4.43 us
    conv_general_dilated x5, local copies, waits for them, and re-layouts, conv_layer(): lax.conv_general_dilated(inputs, kernel, (1, 1), 'VALID', dimension_numbe...  4.36 us
    slice x8, local copies, waits for them, and re-layouts, advect(): nearby[offset] = jnp.roll(middle, -offset, axis=3)  3.83 us
    all_to_all x1, starting transfers between devices, on_device(): lax.all_to_all(block_final, 'gx', split_axis=3, concat_axis=2, tiled=True)  3.5 us
  transfers between devices with their start and end apart: 10, of which 3 were waited for; matrix products, arithmetic and copies ran while one was open for 49% of the time, Pallas kernels for 0%

commit v1 on v0

--- a/solution.py
+++ b/solution.py
@@ -167,9 +167,15 @@
     )
     unused_grad, grad_first = pull_first(middle_grad)
     weight_grads = (grad_first + grad_second).astype(jnp.bfloat16)
-    final_state = jnp.swapaxes(
-        lax.all_to_all(block_final, "gx", split_axis=3, concat_axis=2, tiled=True), 2, 3
-    )
+
+    def _set_shards(piece_in, axis_id, dim_at, join_dim=2):
+        piece_now = jnp.stack(jnp.split(piece_in, lax.axis_size(axis_id), dim_at), axis=0)
+        later = jnp.concatenate(
+            lax.all_to_all(piece_now, concat_axis=0, split_axis=0, axis_name=axis_id), join_dim
+        )
+        return later
+
+    final_state = jnp.swapaxes(_set_shards(block_final, "gx", 3), 2, 3)
     return (final_state, weight_grads)
 
 

time: 86.4 us -> 86.3 us (level)
    all_to_all x2 -> x0, local copies, waits for them, and re-layouts: 1.41 us -> none  [on_device(): lax.all_to_all(block_final, 'gx', split_axis=3, concat_axis=2, tiled=True)]
    reshape x0 -> x2, local copies, waits for them, and re-layouts: none -> 1.34 us  [_set_shards(): jnp.concatenate(lax.all_to_all(piece_now, concat_axis=0, split_axis=0, ax...]
    unnamed x60 -> x75, local copies, waits for them, and re-layouts: 7.5 us -> 7.73 us
  transfers between devices with their start and end apart: 10 -> 10, of which waited for: 3 -> 3; matrix products, arithmetic and copies ran while one was open for 49% -> 50% of each run, Pallas kernels for 0% -> 0%
where the time goes in v1:
time: 86.3 us; the launch traced here: 85.4 us
  local copies, waits for them, and re-layouts  26.1 us (30%)
  starting transfers between devices  24.5 us (28%)
  other arithmetic  13.9 us (16%)
  matrix products  11.3 us (13%)
  waiting for transfers between devices  8.24 us (10%)
  between operations  1.43 us (2%)
    ppermute x4, starting transfers between devices, with_halo(): after = lax.ppermute(leading, axis, down)  14.5 us
    conv_general_dilated x3, matrix products, conv_layer(): lax.conv_general_dilated(inputs, kernel, (1, 1), 'VALID', dimension_numbe...  11.3 us
    unnamed x75, local copies, waits for them, and re-layouts  7.73 us
    all_to_all x1, starting transfers between devices, on_device(): lax.all_to_all(cotangent, 'gx', split_axis=3, concat_axis=2, tiled=True)  5.86 us
    ppermute x4, waiting for transfers between devices, with_halo(): before = lax.ppermute(last, axis, up)  4.43 us
    conv_general_dilated x5, local copies, waits for them, and re-layouts, conv_layer(): lax.conv_general_dilated(inputs, kernel, (1, 1), 'VALID', dimension_numbe...  4.36 us
    slice x8, local copies, waits for them, and re-layouts, advect(): nearby[offset] = jnp.roll(middle, -offset, axis=3)  3.83 us
    all_to_all x1, starting transfers between devices, _set_shards(): lax.all_to_all(piece_now, concat_axis=0, split_axis=0, axis_name=axis_id)  3.5 us
  transfers between devices with their start and end apart: 10, of which 3 were waited for; matrix products, arithmetic and copies ran while one was open for 50% of the time, Pallas kernels for 0%

profile of v1, /device:TPU:0, one launch (start us, length us, event | category | flops | bytes accessed | tf_op | source)
XLA Modules:
  0.0 85.4 jit_solution(15190325078244359014)
XLA Ops:
  0.7 0.8 fusion.159
  2.0 5.1 %collective-permute-start.1 = (bf16[3,4,3,128]{3,2,1,0:T(4,128)(2,1)S(1)}, bf16[3,4,3,128]{3,2,1,0:T(4,128)(2,1)S(1)}, u32[]{:S(2)}, u32[]{:S(2)}) collective-permute-start(bf16[3,4,3,128]{3,2,1,0:T(4,128)(2,1)S(1)} %get-tuple-element.171), channel_id=1, source_target_pairs={{1,0},{2,1},{3,2},{4,3},{5,4},{6,5},{7,6},{8,7},{9,8},{10,9},{11,1... | collective-permute-start | bytes 27656 | tf_op jit(solution)/shard_map/ppermute | solution.py:21
  7.1 1.5 %fusion.157 = (f32[3,8,2,128]{3,2,1,0:T(2,128)}, f32[3,8,2,128]{3,2,1,0:T(2,128)}) fusion(bf16[3,8,8,128]{3,2,1,0:T(8,128)(2,1)} %param.7), kind=kLoop, calls=%fused_computation.357 | loop fusion | bytes 98304 | tf_op jit(solution)/shard_map/slice | solution.py:19
  9.3 1.1 %copy.102 = f32[3,4,8,128]{2,1,0,3:T(4,128)S(1)} copy(f32[3,4,8,128]{3,2,1,0:T(8,128)} %param.12) | data formatting | bytes 98304 | tf_op args[5]
  10.4 1.4 %reshape.466 = f32[16,1,768]{2,1,0:T(1,128)} reshape(f32[128,3,4,8]{3,2,1,0:T(4,128)S(1)} %bitcast.528) | data formatting | bytes 98304
  11.8 5.9 %all-to-all-start.1 = ((f32[16,1,768]{2,1,0:T(1,128)}), f32[16,1,768]{2,1,0:T(1,128)}, u32[]{:S(2)}, u32[]{:S(2)}) async-start(f32[16,1,768]{2,1,0:T(1,128)} %reshape.466), calls=%async_computation.1 | async-start | bytes 98304 | tf_op jit(solution)/shard_map/all_to_all | solution.py:142
  17.7 0.8 convert_element_type.54
  18.5 1.5 %fusion.160 = (f32[3,4,8,1]{3,2,1,0:T(8,128)}, f32[3,4,8,1]{3,2,1,0:T(8,128)S(1)}) fusion(bf16[3,8,8,128]{3,2,1,0:T(8,128)(2,1)} %param.7), kind=kLoop, calls=%fused_computation.360 | loop fusion | bytes 1536 | tf_op jit(solution)/shard_map/jvp(jit(_roll_static))/slice | solution.py:110
  28.6 0.8 reshape.448
  30.4 1.9 %copy.86 = bf16[9,14,32,19]{2,0,3,1:T(8,128)(2,1)S(1)} copy(bf16[9,14,32,19]{3,2,1,0:T(8,128)(2,1)S(1)} %fusion.36) | data formatting | bytes 306432 | tf_op jit(solution)/shard_map/conv_general_dilated | solution.py:71
  32.3 4.4 %select_bitcast_fusion = bf16[12,4,8,17,64]{4,2,1,3,0:T(8,128)(2,1)S(1)} fusion(pred[32,17]{0,1:T(8,128)(4,1)S(1)} %copy-done.23, bf16[9,14,32,19]{2,0,3,1:T(8,128)(2,1)S(1)} %copy.86, bf16[64,9,3,3]{0,3,2,1:T(4,128)(2,1)} %param.9), kind=kOutput, calls=%fused_computation.30 | convolution fusion | flops 72278016 | bytes 999712 | tf_op jit(solution)/shard_map/conv_general_dilated | solution.py:71
  36.9 4.0 %select_bitcast_fusion.1 = bf16[10,4,8,17,64]{4,2,1,3,0:T(8,128)(2,1)S(1)} fusion(pred[32,17]{0,1:T(8,128)(4,1)S(1)} %copy-done.22, bf16[64,64,3,3]{1,0,3,2:T(8,128)(2,1)S(1)} %copy-done, bf16[12,4,7,2,64]{4,2,1,3,0:T(8,128)(2,1)S(1)} %slice.444, bf16[12,4,8,17,64]{4,2,1,3,0:T(8,128)(2,1)S(1)} %select_bitcast_fusion), kind=kOutput, calls=%fused_computation.37 | convolution fusion | flops 407363584 | bytes 1692192 | tf_op jit(solution)/shard_map/conv_general_dilated | solution.py:71
  40.9 2.9 %fusion.28 = f32[8,32,17,36]{3,1,2,0:T(8,128)S(1)} fusion(bf16[36,64,3,3]{1,0,3,2:T(8,128)(2,1)S(1)} %copy-done.21, bf16[10,4,7,2,64]{4,2,1,3,0:T(8,128)(2,1)S(1)} %slice.445, bf16[10,4,8,17,64]{4,2,1,3,0:T(8,128)(2,1)S(1)} %select_bitcast_fusion.1), kind=kOutput, calls=%fused_computation.33 | convolution fusion | flops 182820864 | bytes 1436160 | tf_op jit(solution)/shard_map/conv_general_dilated | solution.py:71
  43.8 1.3 %copy.88 = f32[8,32,17,36]{3,0,2,1:T(8,128)S(1)} copy(f32[8,32,17,36]{3,1,2,0:T(8,128)S(1)} %fusion.28) | data formatting | bytes 1253376 | tf_op jit(solution)/shard_map/conv_general_dilated | solution.py:71
  45.2 0.9 %copy.110 = f32[8,4,128,36]{2,0,1,3:T(8,128)S(1)} copy(f32[8,4,128,36]{3,0,2,1:T(8,128)S(1)} %slice.446) | data formatting | bytes 1179648
  46.9 1.3 %broadcast_multiply_fusion.1 = (f32[4,8,128]{2,1,0:T(8,128)S(1)}, f32[4,8,128]{2,1,0:T(8,128)S(1)}, f32[4,8,128]{2,1,0:T(8,128)S(1)}, f32[4,8,128]{2,1,0:T(8,128...) fusion(f32[3,4,8,1]{3,2,1,0:T(8,128)S(1)} %get-tuple-element.173, f32[3,4,8,127]{3,2,1,0:T(8,128)S(1)} %get-tuple-element.175, ...), kind=kLoop, calls=%fused_computation.304 | loop fusion | flops 45056 | bytes 385024 | tf_op jit(solution)/shard_map/transpose(jvp())/mul | solution.py:119
  48.2 0.8 fusion.102
  49.0 1.0 %fusion.73 = f32[3,4,8,128]{3,2,1,0:T(8,128)S(1)} fusion(f32[3,4,8,2]{3,2,1,0:T(8,128)S(1)} %copy-done.5, f32[3,4,8,126]{3,2,1,0:T(8,128)S(1)} %copy-done.7, f32[3,4,8,126]{3,2,1,0:T(8,128)S(1)} %copy-done.6, f32[3,4,8,2]{3,2,1,0:T(8,128)S(1)} %copy-done.4, f32[3,8,8,128]{3,2,1,0:T(8,128)S(1)} %convert_element_type.54, ...), kind=kLoop, calls=%fused_computation.144 | loop fusion | flops 774144 | bytes 1523712 | tf_op jit(solution)/shard_map/jvp()/sub | solution.py:120
  50.2 4.4 %collective-permute-start.4 = (f32[3,8,2,128]{3,2,1,0:T(2,128)S(1)}, f32[3,8,2,128]{3,2,1,0:T(2,128)S(1)}, u32[]{:S(2)}, u32[]{:S(2)}) collective-permute-start(f32[3,8,2,128]{3,2,1,0:T(2,128)S(1)} %get-tuple-element.111), channel_id=1, source_target_pairs={{1,0},{2,1},{3,2},{4,3},{5,4},{6,5},{7,6},{8,7},{9,8},{10,9},{11,1... | collective-permute-start | bytes 73736 | tf_op jit(solution)/shard_map/ppermute | solution.py:21
  54.7 1.4 %collective-permute-done.4 = f32[3,8,2,128]{3,2,1,0:T(2,128)S(1)} collective-permute-done((f32[3,8,2,128]{3,2,1,0:T(2,128)S(1)}, f32[3,8,2,128]{3,2,1,0:T(2,128)S(1)}, u32[]{:S(2)}, u32[]{:S(2)}) %collective-permute-start.4) | collective-permute-done | bytes 24608 | tf_op jit(solution)/shard_map/ppermute | solution.py:21
  56.2 4.4 %collective-permute-done.5 = f32[3,8,2,128]{3,2,1,0:T(2,128)S(1)} collective-permute-done((f32[3,8,2,128]{3,2,1,0:T(2,128)S(1)}, f32[3,8,2,128]{3,2,1,0:T(2,128)S(1)}, u32[]{:S(2)}, u32[]{:S(2)}) %collective-permute-start.5) | collective-permute-done | bytes 24608 | tf_op jit(solution)/shard_map/ppermute | solution.py:20
  61.2 1.5 %reduce = f32[16,768]{1,0:T(8,128)S(1)} reduce(f32[16,1,768]{2,1,0:T(1,128)} %all-to-all-done.1, f32[]{:T(128)} %broadcast.630), dimensions={1}, to_apply=%all_to_all.17.reduce_sub_computation | reduce | bytes 98308 | tf_op jit(solution)/shard_map/all_to_all | solution.py:142
  62.8 0.9 %reshape.467 = f32[128,3,4,8]{3,2,1,0:T(4,128)S(1)} reshape(f32[16,768]{1,0:T(8,128)S(1)} %reduce) | data formatting | bytes 98304
  65.8 4.4 %collective-permute-start.7 = (bf16[3,4,2,128]{3,2,1,0:T(2,128)(2,1)S(1)}, bf16[3,4,2,128]{3,2,1,0:T(2,128)(2,1)}, u32[]{:S(2)}, u32[]{:S(2)}) collective-permute-start(bf16[3,4,2,128]{3,2,1,0:T(2,128)(2,1)S(1)} %get-tuple-element.95), channel_id=1, source_target_pairs={{1,0},{2,1},{3,2},{4,3},{5,4},{6,5},{7,6},{8,7},{9,8},{10,9},{11,1... | collective-permute-start | bytes 18440 | tf_op jit(solution)/shard_map/ppermute | solution.py:21
  71.5 1.0 %reshape.464 = f32[16,1,768]{2,1,0:T(1,128)} reshape(f32[16,3,4,8,8]{4,3,2,1,0:T(8,128)S(1)} %fusion.49) | data formatting | bytes 98304
  72.6 3.5 %all-to-all-start = ((f32[16,1,768]{2,1,0:T(1,128)}), f32[16,1,768]{2,1,0:T(1,128)S(1)}, u32[]{:S(2)}, u32[]{:S(2)}) async-start(f32[16,1,768]{2,1,0:T(1,128)} %reshape.464), calls=%async_computation | async-start | bytes 98304 | tf_op jit(solution)/shard_map/all_to_all | solution.py:174
  76.2 0.8 convert_add_fusion
  77.5 0.8 multiply_bitcast_fusion.29
  78.4 0.8 multiply_bitcast_fusion.31
  80.5 2.4 %all-to-all-done = f32[16,1,768]{2,1,0:T(1,128)S(1)} async-done(((f32[16,1,768]{2,1,0:T(1,128)}), f32[16,1,768]{2,1,0:T(1,128)S(1)}, u32[]{:S(2)}, u32[]{:S(2)}) %all-to-all-start) | async-done | bytes 49184 | tf_op jit(solution)/shard_map/all_to_all | solution.py:174
  82.8 0.7 reduce.1
  84.4 0.9 %reshape.445 = f32[3,4,128,8]{2,3,1,0:T(8,128)} reshape(f32[3,4,16,8,8]{3,2,4,1,0:T(8,128)S(1)} %copy.101) | data formatting | bytes 98304 | tf_op jit(solution)/shard_map/reshape | solution.py:173
  (151 shorter events, 18.3 us)
Async XLA Ops:
  0.6 36.2 %copy-start = (bf16[64,64,3,3]{1,0,3,2:T(8,128)(2,1)S(1)}, bf16[64,64,3,3]{1,0,3,2:T(8,128)(2,1)}, u32[]{:S(2)}) copy-start(bf16[64,64,3,3]{1,0,3,2:T(8,128)(2,1)} %param.10) | copy-start | bytes 221188
  0.6 27.0 %copy-start.20 = (f32[4]{0:T(128)S(1)}, f32[4]{0:T(128)}, u32[]{:S(2)}) copy-start(f32[4]{0:T(128)} %constant.69.clone) | copy-start | bytes 52
  0.7 19.4 %copy-start.1 = (bf16[3,8,8,128]{3,2,1,0:T(8,128)(2,1)S(1)}, bf16[3,8,8,128]{3,2,1,0:T(8,128)(2,1)}, u32[]{:S(2)}) copy-start(bf16[3,8,8,128]{3,2,1,0:T(8,128)(2,1)} %param.7) | copy-start | bytes 147460
  0.7 24.2 %copy-start.19 = (s32[3]{0:T(128)S(1)}, s32[3]{0:T(128)}, u32[]{:S(2)}) copy-start(s32[3]{0:T(128)} %param.8) | copy-start | bytes 40
  1.5 26.2 %collective-permute-start = (bf16[3,4,3,128]{3,2,1,0:T(4,128)(2,1)S(1)}, bf16[3,4,3,128]{3,2,1,0:T(4,128)(2,1)S(1)}, u32[]{:S(2)}, u32[]{:S(2)}) collective-permute-start(bf16[3,4,3,128]{3,2,1,0:T(4,128)(2,1)S(1)} %get-tuple-element.170), channel_id=1, source_target_pairs={{0,1},{1,2},{2,3},{3,4},{4,5},{5,6},{6,7},{7,8},{8,9},{9,10},{10,1... | collective-permute-start | bytes 27656 | tf_op jit(solution)/shard_map/ppermute | solution.py:20
  2.0 25.7 %collective-permute-start.1 = (bf16[3,4,3,128]{3,2,1,0:T(4,128)(2,1)S(1)}, bf16[3,4,3,128]{3,2,1,0:T(4,128)(2,1)S(1)}, u32[]{:S(2)}, u32[]{:S(2)}) collective-permute-start(bf16[3,4,3,128]{3,2,1,0:T(4,128)(2,1)S(1)} %get-tuple-element.171), channel_id=1, source_target_pairs={{1,0},{2,1},{3,2},{4,3},{5,4},{6,5},{7,6},{8,7},{9,8},{10,9},{11,1... | collective-permute-start | bytes 27656 | tf_op jit(solution)/shard_map/ppermute | solution.py:21
  8.6 38.3 %collective-permute-start.2 = (f32[3,8,2,128]{3,2,1,0:T(2,128)}, f32[3,8,2,128]{3,2,1,0:T(2,128)}, u32[]{:S(2)}, u32[]{:S(2)}) collective-permute-start(f32[3,8,2,128]{3,2,1,0:T(2,128)} %get-tuple-element.166), channel_id=1, source_target_pairs={{1,0},{2,1},{3,2},{4,3},{5,4},{6,5},{7,6},{8,7},{9,8},{10,9},{11,1... | collective-permute-start | bytes 73736 | tf_op jit(solution)/shard_map/ppermute | solution.py:21
  9.3 38.9 %collective-permute-start.3 = (f32[3,8,2,128]{3,2,1,0:T(2,128)}, f32[3,8,2,128]{3,2,1,0:T(2,128)}, u32[]{:S(2)}, u32[]{:S(2)}) collective-permute-start(f32[3,8,2,128]{3,2,1,0:T(2,128)} %get-tuple-element.167), channel_id=1, source_target_pairs={{0,1},{1,2},{2,3},{3,4},{4,5},{5,6},{6,7},{7,8},{8,9},{9,10},{10,1... | collective-permute-start | bytes 73736 | tf_op jit(solution)/shard_map/ppermute | solution.py:20
  11.8 48.9 %all-to-all-start.1 = ((f32[16,1,768]{2,1,0:T(1,128)}), f32[16,1,768]{2,1,0:T(1,128)}, u32[]{:S(2)}, u32[]{:S(2)}) async-start(f32[16,1,768]{2,1,0:T(1,128)} %reshape.466), calls=%async_computation.1 | async-start | bytes 98304 | tf_op jit(solution)/shard_map/all_to_all | solution.py:142
  29.7 2.6 %copy-start.23 = (pred[32,17]{0,1:T(8,128)(4,1)S(1)}, pred[32,17]{0,1:T(8,128)(4,1)}, u32[]{:S(2)}) copy-start(pred[32,17]{0,1:T(8,128)(4,1)} %constant.230) | copy-start | bytes 1636
  32.3 4.5 %copy-start.22 = (pred[32,17]{0,1:T(8,128)(4,1)S(1)}, pred[32,17]{0,1:T(8,128)(4,1)}, u32[]{:S(2)}) copy-start(pred[32,17]{0,1:T(8,128)(4,1)} %constant.229) | copy-start | bytes 1636
  36.8 4.0 %copy-start.21 = (bf16[36,64,3,3]{1,0,3,2:T(8,128)(2,1)S(1)}, bf16[36,64,3,3]{1,0,3,2:T(8,128)(2,1)}, u32[]{:S(2)}) copy-start(bf16[36,64,3,3]{1,0,3,2:T(8,128)(2,1)} %param.11) | copy-start | bytes 124420
  46.2 2.8 %copy-start.4 = (f32[3,4,8,2]{3,2,1,0:T(8,128)S(1)}, f32[3,4,8,2]{3,2,1,0:T(8,128)}, u32[]{:S(2)}) copy-start(f32[3,4,8,2]{3,2,1,0:T(8,128)} %get-tuple-element.176) | copy-start | bytes 2308
  46.2 2.8 %copy-start.5 = (f32[3,4,8,2]{3,2,1,0:T(8,128)S(1)}, f32[3,4,8,2]{3,2,1,0:T(8,128)}, u32[]{:S(2)}) copy-start(f32[3,4,8,2]{3,2,1,0:T(8,128)} %get-tuple-element.177) | copy-start | bytes 2308
  46.2 2.8 %copy-start.6 = (f32[3,4,8,126]{3,2,1,0:T(8,128)S(1)}, f32[3,4,8,126]{3,2,1,0:T(8,128)}, u32[]{:S(2)}) copy-start(f32[3,4,8,126]{3,2,1,0:T(8,128)} %get-tuple-element.178) | copy-start | bytes 145156
  46.2 2.8 %copy-start.7 = (f32[3,4,8,126]{3,2,1,0:T(8,128)S(1)}, f32[3,4,8,126]{3,2,1,0:T(8,128)}, u32[]{:S(2)}) copy-start(f32[3,4,8,126]{3,2,1,0:T(8,128)} %get-tuple-element.179) | copy-start | bytes 145156
  48.9 7.2 %copy-start.16 = (f32[4,8,128]{2,1,0:T(8,128)}, f32[4,8,128]{2,1,0:T(8,128)S(1)}, u32[]{:S(2)}) copy-start(f32[4,8,128]{2,1,0:T(8,128)S(1)} %get-tuple-element.117) | copy-start | bytes 49156
  50.2 5.9 %collective-permute-start.4 = (f32[3,8,2,128]{3,2,1,0:T(2,128)S(1)}, f32[3,8,2,128]{3,2,1,0:T(2,128)S(1)}, u32[]{:S(2)}, u32[]{:S(2)}) collective-permute-start(f32[3,8,2,128]{3,2,1,0:T(2,128)S(1)} %get-tuple-element.111), channel_id=1, source_target_pairs={{1,0},{2,1},{3,2},{4,3},{5,4},{6,5},{7,6},{8,7},{9,8},{10,9},{11,1... | collective-permute-start | bytes 73736 | tf_op jit(solution)/shard_map/ppermute | solution.py:21
  54.7 6.0 %collective-permute-start.5 = (f32[3,8,2,128]{3,2,1,0:T(2,128)S(1)}, f32[3,8,2,128]{3,2,1,0:T(2,128)S(1)}, u32[]{:S(2)}, u32[]{:S(2)}) collective-permute-start(f32[3,8,2,128]{3,2,1,0:T(2,128)S(1)} %get-tuple-element.110), channel_id=1, source_target_pairs={{0,1},{1,2},{2,3},{3,4},{4,5},{5,6},{6,7},{7,8},{8,9},{9,10},{10,1... | collective-permute-start | bytes 73736 | tf_op jit(solution)/shard_map/ppermute | solution.py:20
  65.7 11.4 %copy-start.17 = (f32[4,8,128]{2,1,0:T(8,128)S(1)}, f32[4,8,128]{2,1,0:T(8,128)}, u32[]{:S(2)}) copy-start(f32[4,8,128]{2,1,0:T(8,128)} %copy-done.16) | copy-start | bytes 49156
  65.7 10.5 %collective-permute-start.6 = (bf16[3,4,2,128]{3,2,1,0:T(2,128)(2,1)S(1)}, bf16[3,4,2,128]{3,2,1,0:T(2,128)(2,1)}, u32[]{:S(2)}, u32[]{:S(2)}) collective-permute-start(bf16[3,4,2,128]{3,2,1,0:T(2,128)(2,1)S(1)} %get-tuple-element.94), channel_id=1, source_target_pairs={{0,1},{1,2},{2,3},{3,4},{4,5},{5,6},{6,7},{7,8},{8,9},{9,10},{10,1... | collective-permute-start | bytes 18440 | tf_op jit(solution)/shard_map/ppermute | solution.py:20
  65.8 10.4 %collective-permute-start.7 = (bf16[3,4,2,128]{3,2,1,0:T(2,128)(2,1)S(1)}, bf16[3,4,2,128]{3,2,1,0:T(2,128)(2,1)}, u32[]{:S(2)}, u32[]{:S(2)}) collective-permute-start(bf16[3,4,2,128]{3,2,1,0:T(2,128)(2,1)S(1)} %get-tuple-element.95), channel_id=1, source_target_pairs={{1,0},{2,1},{3,2},{4,3},{5,4},{6,5},{7,6},{8,7},{9,8},{10,9},{11,1... | collective-permute-start | bytes 18440 | tf_op jit(solution)/shard_map/ppermute | solution.py:21
  70.2 6.9 %copy-start.18 = (f32[4,8,128]{2,1,0:T(8,128)S(1)}, f32[4,8,128]{2,1,0:T(8,128)}, u32[]{:S(2)}) copy-start(f32[4,8,128]{2,1,0:T(8,128)} %get-tuple-element.114) | copy-start | bytes 49156
  70.7 6.6 %copy-start.12 = (f32[3,1,1,4,8,2]{5,4,3,0,2,1:T(8,128)S(1)}, f32[3,1,1,4,8,2]{5,4,3,0,2,1:T(8,128)}, u32[]{:S(2)}) copy-start(f32[3,1,1,4,8,2]{5,4,3,0,2,1:T(8,128)} %get-tuple-element.86) | copy-start | bytes 2308
  70.7 6.6 %copy-start.13 = (f32[3,1,1,4,8,126]{5,4,3,0,2,1:T(8,128)S(1)}, f32[3,1,1,4,8,126]{5,4,3,0,2,1:T(8,128)}, u32[]{:S(2)}) copy-start(f32[3,1,1,4,8,126]{5,4,3,0,2,1:T(8,128)} %get-tuple-element.88) | copy-start | bytes 145156
  70.7 6.6 %copy-start.14 = (f32[3,1,1,4,8,127]{5,4,3,0,2,1:T(8,128)S(1)}, f32[3,1,1,4,8,127]{5,4,3,0,2,1:T(8,128)}, u32[]{:S(2)}) copy-start(f32[3,1,1,4,8,127]{5,4,3,0,2,1:T(8,128)} %get-tuple-element.90) | copy-start | bytes 146308
  70.7 6.6 %copy-start.15 = (f32[3,1,1,4,8,1]{5,4,3,0,2,1:T(8,128)S(1)}, f32[3,1,1,4,8,1]{5,4,3,0,2,1:T(8,128)}, u32[]{:S(2)}) copy-start(f32[3,1,1,4,8,1]{5,4,3,0,2,1:T(8,128)} %get-tuple-element.92) | copy-start | bytes 1156
  71.1 6.3 %copy-start.8 = (f32[3,1,1,4,8,2]{5,4,3,0,2,1:T(8,128)S(1)}, f32[3,1,1,4,8,2]{5,4,3,0,2,1:T(8,128)}, u32[]{:S(2)}) copy-start(f32[3,1,1,4,8,2]{5,4,3,0,2,1:T(8,128)} %get-tuple-element.87) | copy-start | bytes 2308
  71.1 6.3 %copy-start.9 = (f32[3,1,1,4,8,126]{5,4,3,0,2,1:T(8,128)S(1)}, f32[3,1,1,4,8,126]{5,4,3,0,2,1:T(8,128)}, u32[]{:S(2)}) copy-start(f32[3,1,1,4,8,126]{5,4,3,0,2,1:T(8,128)} %get-tuple-element.89) | copy-start | bytes 145156
  71.1 6.3 %copy-start.10 = (f32[3,1,1,4,8,127]{5,4,3,0,2,1:T(8,128)S(1)}, f32[3,1,1,4,8,127]{5,4,3,0,2,1:T(8,128)}, u32[]{:S(2)}) copy-start(f32[3,1,1,4,8,127]{5,4,3,0,2,1:T(8,128)} %get-tuple-element.91) | copy-start | bytes 146308
  71.1 6.3 %copy-start.11 = (f32[3,1,1,4,8,1]{5,4,3,0,2,1:T(8,128)S(1)}, f32[3,1,1,4,8,1]{5,4,3,0,2,1:T(8,128)}, u32[]{:S(2)}) copy-start(f32[3,1,1,4,8,1]{5,4,3,0,2,1:T(8,128)} %get-tuple-element.93) | copy-start | bytes 1156
  72.6 10.2 %all-to-all-start = ((f32[16,1,768]{2,1,0:T(1,128)}), f32[16,1,768]{2,1,0:T(1,128)S(1)}, u32[]{:S(2)}, u32[]{:S(2)}) async-start(f32[16,1,768]{2,1,0:T(1,128)} %reshape.464), calls=%async_computation | async-start | bytes 98304 | tf_op jit(solution)/shard_map/all_to_all | solution.py:174
  (2 other events, 4.1 us)
